TPU v7x, 32 devices: a whole 2x2x4 slice. The times are simulated.
32 devices in a mesh: layout: 4 (over z), gx: 4 (over y, core), gy: 2 (over x).
Axes of the slice: x: 2, y: 2, z: 4, core: 2. Of those that a mesh axis runs over, the one named last changes fastest.
Arguments:
- state: float32 [4, 4, 64, 32, 256], P('layout', None, 'gx', None, 'gy'), may hold values from -2 to 2
- planes: float32 [8, 4, 32, 256], P('layout', None, None, 'gy'), may hold values from -2 to 2
- turbine_cell: int32 [4, 64, 32, 256], P('layout', 'gx', None, 'gy'), may hold values from -1 to 15, as said below
- active: int32 [4, 16], P('layout'), may hold values 0 or 1
- yaw_sector: int32 [4, 16], P('layout'), may hold values from 0 to 7
- slot: int32 [4], replicated, may hold values from 0 to 7
Outputs:
- fields: float32 [4, 4, 64, 32, 256], P('layout', None, 'gx', None, 'gy')
Inputs may be any that keep to these rules, and one draw needn't show every extreme that they name: `turbine_cell`: cells of value t form turbine t's actuator disk: one streamwise cell, 11 levels around level 16 and 11 spanwise cells (periodic). Every turbine has its disk and disks don't intersect; -1 elsewhere.
All inputs are finite; a program needn't handle non-finite values. No bound on the sum of `active` on one device may be relied on, other than what follows from the above.
Results may differ from a plain program's by a relative error of at most 0.00015.
Values sent between devices are 32-bit elements; how exact they have to be, the bound alone decides.
A program may use at most 64 MiB of HBM per device.

v0:
```python
import functools

import jax
import jax.numpy as jnp
from jax import lax
from jax.experimental import pallas as pl
from jax.experimental.pallas import tpu as pltpu
from jax.sharding import PartitionSpec as P

STEPS = 4
SWEEPS = 4
RADIUS = 5

TIME_STEP = 0.25
VISCOSITY = 0.02
SMAGORINSKY = 0.0289
DIFFUSIVITY_RATIO = 1.0 / 0.7
BUOYANCY = 0.5
THRUST_COEFF = 1.33
YAW_INCREMENT = 0.1
MESH = pl.DeviceIdType.MESH


def profiles(levels):
    height = (jnp.arange(levels).astype(jnp.float32) + 0.5) / levels
    return jnp.stack([height ** (1.0 / 7.0), 0.5 * height])


def kernel(
    NL, GX, L, R, K, H, turbines, held, columns,
    slot, table, prof, ids, state, planes,
    out,
    F, G, U, RR, P0, P1, P2, P3, PL, ID, SU, NM, FO, TS, EA, EM, EB, EC, EL,
    i_s, i_r, p_s, p_r, a_s, a_r, b_s, b_r, c_s, c_r, t_s, t_r, loc,
):
    lay = lax.axis_index("layout")
    gx = lax.axis_index("gx")
    gy = lax.axis_index("gy")
    N = GX * L
    s = gx * L + gy
    first = gx == 0
    last = gx == GX - 1
    inner_end = jnp.logical_not(last)
    inner_start = jnp.logical_not(first)
    up_x, down_x = lax.rem(gx + 1, GX), lax.rem(gx + GX - 1, GX)
    up_y, down_y = lax.rem(gy + 1, L), lax.rem(gy + L - 1, L)
    blocks = R // 8
    PP = [P0, P1, P2, P3]

    def device_of(t):
        return {"gx": t // L, "gy": lax.rem(t, L)}

    barrier = pltpu.get_barrier_semaphore()
    for d in range(1, N):
        pl.semaphore_signal(barrier, inc=1, device_id=device_of(lax.rem(s + d, N)), device_id_type=MESH)

    @pl.when(first)
    def _():
        for d in range(1, NL):
            pl.semaphore_signal(
                barrier, inc=1, device_id={"layout": lax.rem(lay + d, NL)}, device_id_type=MESH
            )

    own_state = pltpu.make_async_copy(state.at[0], F.at[:, pl.ds(1, R)], loc.at[0])
    own_planes = pltpu.make_async_copy(planes, PL.at[pl.ds(lay * held, held)], loc.at[1])
    own_state.start()

    @pl.when(first)
    def _():
        own_planes.start()

    zero = jnp.zeros((2, K, 128), jnp.float32)
    for buf in [RR] + PP:
        @pl.when(first)
        def _():
            def body(i, c):
                buf[i] = zero
                return c
            lax.fori_loop(0, H, body, 0)

        @pl.when(last)
        def _():
            def body(i, c):
                buf[R + H + i] = zero
                return c
            lax.fori_loop(0, H, body, 0)

    ID[0] = ids[...]

    pl.semaphore_wait(barrier, N - 1 + jnp.where(first, NL - 1, 0))

    class Exchange:
        def __init__(self, send, recv):
            self.send, self.recv, self.items = send, recv, []

        def add(self, src, dst, device, out_if=None, in_if=None):
            i = len(self.items)

            def copy():
                return pltpu.make_async_remote_copy(
                    src_ref=src, dst_ref=dst, send_sem=self.send.at[i], recv_sem=self.recv.at[i],
                    device_id=device, device_id_type=MESH)

            self.items.append((copy, out_if, in_if))
            return self

        def rows(self, up_src, up_dst, down_src, down_dst):
            self.add(up_src, up_dst, {"gx": up_x}, inner_end, inner_start)
            return self.add(down_src, down_dst, {"gx": down_x}, inner_start, inner_end)

        def span(self, src, dst_above, dst_below):
            self.add(src, dst_above, {"gy": up_y})
            return self.add(src, dst_below, {"gy": down_y})

        def start(self, which=slice(None)):
            for copy, out_if, _ in self.items[which]:
                if out_if is None:
                    copy().start()
                else:
                    pl.when(out_if)(lambda: copy().start())

        def wait(self):
            for copy, out_if, in_if in self.items:
                if out_if is None:
                    copy().wait()
                else:
                    pl.when(out_if)(lambda: copy().wait_send())
                    pl.when(in_if)(lambda: copy().wait_recv())

    def ids_exchange():
        return Exchange(i_s, i_r).span(ID.at[0], ID.at[1], ID.at[2])

    def fields_exchange():
        e = Exchange(a_s, a_r).rows(F.at[:, R], F.at[:, 0], F.at[:, 1], F.at[:, R + 1])
        return e.span(EA.at[0], EA.at[1], EA.at[2]).span(NM.at[0], NM.at[1], NM.at[2])

    def speed_exchange():
        e = Exchange(b_s, b_r).rows(U.at[R], U.at[0], U.at[1], U.at[R + 1])
        return e.span(EB.at[0], EB.at[1], EB.at[2])

    def source_exchange():
        e = Exchange(c_s, c_r).rows(
            RR.at[pl.ds(R, H), 0], RR.at[pl.ds(0, H), 0],
            RR.at[pl.ds(H, H), 0], RR.at[pl.ds(H + R, H), 0])
        e.span(EC, EL.at[0, pl.ds(1, blocks)], EL.at[1, pl.ds(1, blocks)])
        for side, to in ((0, up_y), (1, down_y)):
            e.add(EC.at[blocks - 1], EL.at[side, 0], {"gx": up_x, "gy": to}, inner_end, inner_start)
            e.add(EC.at[0], EL.at[side, blocks + 1], {"gx": down_x, "gy": to}, inner_start, inner_end)
        return e

    def planes_copy(d):
        return pltpu.make_async_remote_copy(
            src_ref=planes, dst_ref=PL.at[pl.ds(lay * held, held)],
            send_sem=p_s.at[d], recv_sem=p_r.at[d],
            device_id={"layout": lax.rem(lay + d, NL)}, device_id_type=MESH,
        )

    def planes_landing(d):
        source = lax.rem(lay + NL - d, NL)
        return pltpu.make_async_remote_copy(
            src_ref=planes, dst_ref=PL.at[pl.ds(source * held, held)],
            send_sem=p_s.at[d], recv_sem=p_r.at[d],
            device_id={"layout": source}, device_id_type=MESH,
        )

    ids_exchange().start()

    @pl.when(first)
    def _():
        for d in range(1, NL):
            planes_copy(d).start()

    lane = lax.broadcasted_iota(jnp.int32, (K, 128), 1)
    level = lax.broadcasted_iota(jnp.int32, (K, 128), 0)
    at_first, at_last = lane == 0, lane == 127
    odd_lane = lax.rem(lane, 2) == 1
    at_floor, at_top = level == 0, level == K - 1
    low = K // 2 - RADIUS
    in_band = (level >= low) & (level <= low + 2 * RADIUS)

    def beside_y(f, rim):
        before = pltpu.roll(jnp.where(at_last, rim, f), 1, 1)
        after = pltpu.roll(jnp.where(at_first, rim, f), 127, 1)
        return before, after

    def beside_k(f, keep=True):
        edge = f if keep else jnp.zeros_like(f)
        below = jnp.where(at_floor, edge, pltpu.roll(f, 1, 0))
        above = jnp.where(at_top, edge, pltpu.roll(f, K - 1, 0))
        return below, above

    def pack(packed, f, j, width):
        return jnp.where(lane // width == j, pltpu.roll(f, width * j + width // 2, 1), packed)

    def unpack(packed, j, width):
        return pltpu.roll(packed, 128 - width // 2 - width * j, 1)

    own_ids = ID[0]
    cosines = jnp.zeros((R, 128), jnp.float32)
    sines, runs = cosines, cosines
    for t in range(turbines):
        here = own_ids == t
        cosines = jnp.where(here, table[0, t], cosines)
        sines = jnp.where(here, table[1, t], sines)
        runs = jnp.where(here, table[2, t], runs)
    FO[2] = cosines
    FO[3] = sines
    FO[4] = runs

    def disk_forces():
        lane_r = lax.broadcasted_iota(jnp.int32, (R, 128), 1)
        names = [ID[i] for i in range(3)]
        normal = [NM[i] for i in range(3)]
        total = normal[0]
        for shift in range(1, 2 * RADIUS + 1):
            for other, amount, wraps in (
                (1, shift, lane_r >= 128 - shift), (2, 128 - shift, lane_r < shift)
            ):
                n_sh = pltpu.roll(jnp.where(wraps, normal[other], normal[0]), amount, 1)
                i_sh = pltpu.roll(jnp.where(wraps, names[other], names[0]), amount, 1)
                total = total + jnp.where(i_sh == names[0], n_sh, 0.0)
        speed = total / float((2 * RADIUS + 1) ** 2)
        thrust = -0.5 * THRUST_COEFF * speed * jnp.abs(speed) * FO[4]
        FO[0] = thrust * FO[2]
        FO[1] = thrust * FO[3]

    def disk_sums(row, u, v):
        SU[0, row:row + 1, :] = jnp.sum(jnp.where(in_band, u, 0.0), axis=0, keepdims=True)
        SU[1, row:row + 1, :] = jnp.sum(jnp.where(in_band, v, 0.0), axis=0, keepdims=True)

    def send_span():
        NM[0] = SU[0] * FO[2] + SU[1] * FO[3]
        fields_exchange().start(slice(2, None))

    groups = K // 8
    width = 128 // groups
    lane_8 = lax.broadcasted_iota(jnp.int32, (8, 128), 1)

    def theta_copy(par, d):
        return pltpu.make_async_remote_copy(
            src_ref=TS.at[par, 0], dst_ref=TS.at[par, d],
            send_sem=t_s.at[par, d], recv_sem=t_r.at[par, d],
            device_id=device_of(lax.rem(s + d, N)), device_id_type=MESH,
        )

    def send_theta(par, total):
        packed = jnp.zeros((8, 128), jnp.float32)
        for g in range(groups):
            part = jnp.sum(total[g * 8:(g + 1) * 8], axis=1, keepdims=True)
            packed = jnp.where(lane_8 // width == g, part, packed)
        TS[par, 0] = packed
        for d in range(1, N):
            theta_copy(par, d).start()

    def mean_theta(par):
        for d in range(1, N):
            theta_copy(par, d).wait()
        total = TS[par, 0]
        for d in range(1, N):
            total = total + TS[par, d]
        total = total / columns
        return jnp.concatenate(
            [jnp.broadcast_to(total[:, g * width:g * width + 1], (8, 128)) for g in range(groups)], axis=0
        )

    own_state.wait()

    total = jnp.zeros((K, 128), jnp.float32)
    packed = zero[0]
    for row in range(R):
        u = F[0, row + 1] + prof[0]
        v = F[1, row + 1]
        warm = F[3, row + 1] + prof[1]
        F[0, row + 1] = u
        F[3, row + 1] = warm
        disk_sums(row, u, v)
        for c, f in enumerate((u, v, F[2, row + 1], warm)):
            packed = pack(packed, f, c * R + row, 2)
        total = total + warm
    EA[0] = packed
    fields_exchange().start(slice(0, 2))
    send_span()
    send_theta(0, total)
    ids_exchange().wait()

    @pl.when(first)
    def _():
        own_planes.wait()
        for d in range(1, NL):
            planes_copy(d).wait_send()
            planes_landing(d).wait_recv()

    def tendency_row(row, carry):
        x = row + 1
        rims = EM[...]
        cen, dx, dy, dz, lap = [], [], [], [], []
        for c in range(4):
            f = F[c, x]
            xm, xp = F[c, x - 1], F[c, x + 1]
            ym, yp = beside_y(f, unpack(rims, c * R + row, 2))
            km, kp = beside_k(f, c != 2)
            cen.append(f)
            dx.append(xp - xm)
            dy.append(yp - ym)
            dz.append(kp - km)
            lap.append((xp + xm) + (kp + km) + (yp + ym) - 6.0 * f)
        square = 2.0 * (dx[0] * dx[0] + dy[1] * dy[1] + dz[2] * dz[2])
        for shear in (dy[0] + dx[1], dz[0] + dx[2], dz[1] + dy[2]):
            square = square + shear * shear
        nu = VISCOSITY + (0.5 * SMAGORINSKY) * jnp.sqrt(square)
        half_u, half_v, half_w = 0.5 * cen[0], 0.5 * cen[1], 0.5 * cen[2]
        for c in range(4):
            visc = nu if c < 3 else nu * DIFFUSIVITY_RATIO
            tend = lap[c] * visc - (half_u * dx[c] + half_v * dy[c] + half_w * dz[c])
            if c < 2:
                force = FO[c, pl.ds(row, 1), :]
                tend = tend + jnp.where(in_band, jnp.broadcast_to(force, (K, 128)), 0.0)
            elif c == 2:
                tend = tend + BUOYANCY * cen[3]
            new = cen[c] + TIME_STEP * tend
            if c == 0:
                U[x] = new
            else:
                G[c - 1, row] = new
        return carry

    def pack_speed():
        packed = zero[0]
        for row in range(R):
            packed = pack(packed, G[0, row], row, 2)
        EB[0] = packed

    def sources(mean):
        rims = jnp.where(odd_lane, EB[2], EB[1])
        lift = (TIME_STEP * BUOYANCY) * mean
        for b in range(blocks):
            packed = zero[0]
            for j in range(8):
                row = 8 * b + j
                vm, vp = beside_y(G[0, row], unpack(rims, row, 2))
                w = G[1, row] - lift
                G[1, row] = w
                wm, wp = beside_k(w, False)
                r = ((U[row + 2] - U[row]) + (vp - vm) + (wp - wm)) * 0.5
                RR[row + H, 0] = r
                packed = pack(packed, r, j, 16)
            EC[b] = packed
            if b == 0:
                source_exchange().start(slice(1, 2))

    def rims():
        right_half = lax.rem(lane, 16) >= 8

        def block(b, items):
            merged = jnp.where(right_half, EL[1, b], EL[0, b])
            for j in items:
                RR[8 * (b - 1) + j + H, 1] = unpack(merged, j, 16)

        pl.when(inner_start)(lambda: block(0, range(8 - H, 8)))
        for b in range(1, blocks + 1):
            block(b, range(8))
        pl.when(inner_end)(lambda: block(blocks + 1, range(H)))

    def sweep(index, v):
        old = RR if index == 0 else PP[index - 1]
        sixth = jnp.float32(1.0 / 6.0)
        at_start = jnp.where(first, 0.0, sixth).astype(jnp.float32)
        at_end = jnp.where(last, 0.0, sixth).astype(jnp.float32)
        for x in range(H - (v - 1), R + H + (v - 1)):
            keep = at_start if x < H else at_end if x >= R + H else sixth
            tiles = [old[x, l] for l in range(2)]
            for l in range(2):
                ym, yp = beside_y(tiles[l], tiles[1 - l])
                km, kp = beside_k(tiles[l])
                around = (old[x + 1, l] + old[x - 1, l]) + (ym + yp) + (km + kp)
                if index == 0:
                    new = (around * (-1.0 / 6.0) - tiles[l]) * keep
                else:
                    new = (around - RR[x, l]) * keep
                PP[index][x, l] = new

    def finish():
        p = PP[SWEEPS - 1]
        total = zero[0]
        packed = zero[0]
        for row in range(R):
            x = row + H
            centre = p[x, 0]
            ym, yp = beside_y(centre, p[x, 1])
            km, kp = beside_k(centre)
            u = U[row + 1] - 0.5 * (p[x + 1, 0] - p[x - 1, 0])
            v = G[0, row] - 0.5 * (yp - ym)
            w = G[1, row] - 0.5 * (kp - km)
            warm = G[2, row]
            disk_sums(row, u, v)
            for c, f in enumerate((u, v, w, warm)):
                F[c, row + 1] = f
                packed = pack(packed, f, c * R + row, 2)
            total = total + warm
        EA[0] = packed
        return total

    def step(n, carry):
        par = lax.rem(n, 2)

        @pl.when(first)
        def _():
            plane = slot[n]
            for c in range(4):
                f = PL[plane, c]
                if c in (0, 3):
                    f = f + prof[0 if c == 0 else 1]
                F[c, 0] = f
                if c == 0:
                    U[0] = f

        @pl.when(last)
        def _():
            for c in range(4):
                F[c, R + 1] = F[c, R]

        fields_exchange().wait()
        EM[...] = jnp.where(odd_lane, EA[2], EA[1])
        disk_forces()
        lax.fori_loop(0, R // 2, lambda i, c: tendency_row(2 * i + 1, tendency_row(2 * i, c)), 0)
        pack_speed()

        @pl.when(last)
        def _():
            U[R + 1] = U[R]

        speed_exchange().start()
        mean = mean_theta(par)
        speed_exchange().wait()
        sources(mean)

        source_exchange().start(slice(2, None))
        source_exchange().start(slice(0, 1))
        source_exchange().wait()
        rims()
        for i in range(SWEEPS):
            sweep(i, H - i)

        total = finish()

        @pl.when(n < STEPS - 1)
        def _():
            fields_exchange().start(slice(0, 2))
            send_span()
            send_theta(1 - par, total)

        return carry

    lax.fori_loop(0, STEPS, step, 0)

    own_out = pltpu.make_async_copy(F.at[:, pl.ds(1, R)], out.at[0], loc.at[2])
    own_out.start()
    own_out.wait()


def solution(mesh):
    NL, GX, L = mesh.shape["layout"], mesh.shape["gx"], mesh.shape["gy"]

    def local(state, planes, turbine_cell, active, yaw_sector, slot):
        rows, K, cols = state.shape[2:]
        R = rows
        H = SWEEPS + 1
        N = GX * L
        turbines = active.shape[1]
        held = planes.shape[0]
        ids = turbine_cell[0, :, K // 2, :]
        angle = (yaw_sector[0].astype(jnp.float32) - 3.5) * YAW_INCREMENT
        table = jnp.stack([jnp.cos(angle), jnp.sin(angle), active[0].astype(jnp.float32)])
        prof = jnp.broadcast_to(profiles(K)[:, :, None], (2, K, cols))
        smem = pl.BlockSpec(memory_space=pltpu.SMEM)
        vmem = pl.BlockSpec(memory_space=pltpu.VMEM)
        hbm = pl.BlockSpec(memory_space=pl.ANY)
        f32 = jnp.float32
        dma = pltpu.SemaphoreType.DMA
        return pl.pallas_call(
            functools.partial(
                kernel, NL, GX, L, R, K, H, turbines, held, float(rows * GX * cols * L)
            ),
            out_shape=jax.ShapeDtypeStruct(state.shape, f32),
            in_specs=[smem, smem, vmem, vmem, hbm, hbm],
            out_specs=hbm,
            scratch_shapes=[
                pltpu.VMEM((4, R + 2, K, cols), f32),
                pltpu.VMEM((3, R, K, cols), f32),
                pltpu.VMEM((R + 2, K, cols), f32),
                pltpu.VMEM((R + 2 * H, 2, K, cols), f32),
                pltpu.VMEM((R + 2 * H, 2, K, cols), f32),
                pltpu.VMEM((R + 2 * H, 2, K, cols), f32),
                pltpu.VMEM((R + 2 * H, 2, K, cols), f32),
                pltpu.VMEM((R + 2 * H, 2, K, cols), f32),
                pltpu.VMEM((held * NL, 4, K, cols), f32),
                pltpu.VMEM((3, R, cols), jnp.int32),
                pltpu.VMEM((2, R, cols), f32),
                pltpu.VMEM((3, R, cols), f32),
                pltpu.VMEM((5, R, cols), f32),
                pltpu.VMEM((2, N, 8, 128), f32),
                pltpu.VMEM((3, K, cols), f32),
                pltpu.VMEM((K, cols), f32),
                pltpu.VMEM((3, K, cols), f32),
                pltpu.VMEM((R // 8, K, cols), f32),
                pltpu.VMEM((2, R // 8 + 2, K, cols), f32),
                dma((2,)), dma((2,)), dma((NL,)), dma((NL,)),
                dma((6,)), dma((6,)), dma((4,)), dma((4,)), dma((8,)), dma((8,)),
                dma((2, N)), dma((2, N)),
                dma((3,)),
            ],
            compiler_params=pltpu.CompilerParams(
                collective_id=0, has_side_effects=True, vmem_limit_bytes=40 * 1024 * 1024
            ),
        )(slot, table, prof, ids, state, planes)

    return jax.shard_map(
        local,
        mesh=mesh,
        in_specs=(
            P("layout", None, "gx", None, "gy"),
            P("layout", None, None, "gy"),
            P("layout", "gx", None, "gy"),
            P("layout", None),
            P("layout", None),
            P(),
        ),
        out_specs=P("layout", None, "gx", None, "gy"),
        check_vma=False,
    )
```

profile of v0, /device:TPU:1, one launch (start us, length us, event | category | flops | bytes accessed | tf_op | source)
XLA Modules:
  0.0 78.6 jit_solution(2743991366819559316)
XLA Ops:
  0.0 0.0 copy-start.3
  0.0 0.7 convert_element_type.26
  0.7 0.0 copy-done.3
  0.8 0.8 %slice.3 = s32[1,16,1,128]{3,2,1,0:T(1,128)S(1)} slice(s32[1,16,32,128]{3,2,1,0:T(8,128)} %param.8), slice={[0:1], [0:16], [16:17], [0:128]} | slice | bytes 16384 | tf_op jit(solution)/shard_map/slice | solution.py:471
  1.6 0.0 copy-start.2
  1.6 0.1 broadcast_in_dim.2.prof
  1.7 0.6 copy-done.2
  2.3 0.0 copy-start
  2.3 1.2 %copy-done = f32[1,4,16,32,128]{4,3,2,1,0:T(8,128)S(1)} copy-done((f32[1,4,16,32,128]{4,3,2,1,0:T(8,128)S(1)}, f32[1,4,16,32,128]{4,3,2,1,0:T(8,128)}, u32[]{:S(2)}) %copy-start) | copy-done | bytes 1048600
  3.5 0.0 copy-start.1
  3.5 0.9 %copy-done.1 = f32[2,4,32,128]{3,2,1,0:T(8,128)S(1)} copy-done((f32[2,4,32,128]{3,2,1,0:T(8,128)S(1)}, f32[2,4,32,128]{3,2,1,0:T(8,128)}, u32[]{:S(2)}) %copy-start.1) | copy-done | bytes 131096
  4.4 73.2 %shard_map.64 = f32[1,4,16,32,128]{4,3,2,1,0:T(8,128)S(1)} custom-call(s32[4]{0:T(128)S(1)} %copy-done.2, f32[3,16]{1,0:T(4,128)S(1)} %pad_maximum_fusion.table, f32[2,32,128]{2,1,0:T(8,128)S(1)} %broadcast_in_dim.2.prof, s32[16,128]{1,0:T(8,128)S(1)} %bitcast.3, f32[1,4,16,32,128]{4,3,2,1,0:T(8,128)S(1)} %copy-done, f32[2,4,32,128]{3,2,1,0:T(8,128)S(1)} %copy-done.1), custom_call_target="tpu_custom_call" | custom-call | tf_op jit(solution)/shard_map/pallas_call | solution.py:480
  77.6 1.0 %copy.10 = f32[1,4,16,32,128]{4,3,2,1,0:T(8,128)} copy(f32[1,4,16,32,128]{4,3,2,1,0:T(8,128)S(1)} %shard_map.64) | data formatting | bytes 2097152
  (4 shorter events, 0.1 us)
Async XLA Ops:
  0.0 0.7 copy-start.3
  1.6 0.7 copy-start.2
  2.3 1.2 %copy-start = (f32[1,4,16,32,128]{4,3,2,1,0:T(8,128)S(1)}, f32[1,4,16,32,128]{4,3,2,1,0:T(8,128)}, u32[]{:S(2)}) copy-start(f32[1,4,16,32,128]{4,3,2,1,0:T(8,128)} %state.1) | copy-start | bytes 3145732
  3.5 0.9 %copy-start.1 = (f32[2,4,32,128]{3,2,1,0:T(8,128)S(1)}, f32[2,4,32,128]{3,2,1,0:T(8,128)}, u32[]{:S(2)}) copy-start(f32[2,4,32,128]{3,2,1,0:T(8,128)} %planes.1) | copy-start | bytes 393220
where the time goes:
time: 78.8 us; the launch traced here: 78.6 us
  Pallas kernels  73.2 us (93%)
  local copies, waits for them, and re-layouts  4.61 us (6%)
    pallas_call x1, Pallas kernels, local(): pl.pallas_call(functools.partial(kernel, NL, GX, L, R, K, H, turbines, he...  73.2 us
    unnamed x9, local copies, waits for them, and re-layouts  3.69 us

commit v1 on v0

v1 whole, which is shorter than its diff:
```python
import functools

import jax
import jax.numpy as jnp
from jax import lax
from jax.experimental import pallas as pl
from jax.experimental.pallas import tpu as pltpu
from jax.sharding import PartitionSpec as P

STEPS = 4
SWEEPS = 4
RADIUS = 5

TIME_STEP = 0.25
VISCOSITY = 0.02
SMAGORINSKY = 0.0289
DIFFUSIVITY_RATIO = 1.0 / 0.7
BUOYANCY = 0.5
THRUST_COEFF = 1.33
YAW_INCREMENT = 0.1
MESH = pl.DeviceIdType.MESH


def profiles(levels):
    height = (jnp.arange(levels).astype(jnp.float32) + 0.5) / levels
    return jnp.stack([height ** (1.0 / 7.0), 0.5 * height])


def kernel(
    NL, GX, L, R, K, H, turbines, held, columns,
    slot, table, prof, ids, state, planes,
    out,
    F, T, TH, NU, V, W, U, RR, PA, PB, SR, SA, SB, PL, ID, SU, NM, FO, MK, TS, EA, EM, MB, OC, EC, EL, XE,
    i_s, i_r, p_s, p_r, a_s, a_r, b_s, b_r, c_s, c_r, t_s, t_r, loc,
):
    lay = lax.axis_index("layout")
    gx = lax.axis_index("gx")
    gy = lax.axis_index("gy")
    N = GX * L
    s = gx * L + gy
    first = gx == 0
    last = gx == GX - 1
    inner_end = jnp.logical_not(last)
    inner_start = jnp.logical_not(first)
    up_x, down_x = lax.rem(gx + 1, GX), lax.rem(gx + GX - 1, GX)
    up_y, down_y = lax.rem(gy + 1, L), lax.rem(gy + L - 1, L)
    blocks = R // 8
    tiles = blocks + 2
    groups = K // 8
    mid = pl.ds(8, K)
    sides = 1 if L == 2 else 2
    PP = [PA, PB]
    SS = [SA, SB]

    def device_of(t):
        return {"gx": t // L, "gy": lax.rem(t, L)}

    barrier = pltpu.get_barrier_semaphore()
    for d in range(1, N):
        pl.semaphore_signal(barrier, inc=1, device_id=device_of(lax.rem(s + d, N)), device_id_type=MESH)

    @pl.when(first)
    def _():
        for d in range(1, NL):
            pl.semaphore_signal(
                barrier, inc=1, device_id={"layout": lax.rem(lay + d, NL)}, device_id_type=MESH
            )

    own_state = pltpu.make_async_copy(state.at[0, pl.ds(0, 3)], F.at[pl.ds(0, 3), pl.ds(1, R), mid], loc.at[0])
    own_theta = pltpu.make_async_copy(state.at[0, 3], T.at[pl.ds(1, R), mid], loc.at[3])
    own_planes = pltpu.make_async_copy(planes, PL.at[pl.ds(lay * held, held)], loc.at[1])
    own_state.start()
    own_theta.start()

    @pl.when(first)
    def _():
        own_planes.start()

    zero = jnp.zeros((K, 128), jnp.float32)

    @pl.when(first)
    def _():
        for i in range(H):
            RR[i, mid] = zero
        for i in range(sides):
            EL[i, 0] = zero
        XE[0] = zero

    @pl.when(last)
    def _():
        for i in range(H):
            RR[R + H + i, mid] = zero
        for i in range(sides):
            EL[i, tiles - 1] = zero
        XE[1] = zero

    no_level = jnp.zeros((8, 128), jnp.float32)
    for row in range(R):
        W[row, 0:8] = no_level
        W[row, 8 + K:16 + K] = no_level
        F[2, row + 1, 0:8] = no_level
        F[2, row + 1, 8 + K:16 + K] = no_level

    ID[0] = ids[...]

    pl.semaphore_wait(barrier, N - 1 + jnp.where(first, NL - 1, 0))

    class Exchange:
        def __init__(self, send, recv):
            self.send, self.recv, self.items = send, recv, []

        def add(self, tag, src, dst, device, out_if=None, in_if=None):
            i = len(self.items)

            def copy():
                return pltpu.make_async_remote_copy(
                    src_ref=src, dst_ref=dst, send_sem=self.send.at[i], recv_sem=self.recv.at[i],
                    device_id=device, device_id_type=MESH)

            self.items.append((tag, copy, out_if, in_if))
            return self

        def rows(self, tag_up, tag_down, up_src, up_dst, down_src, down_dst):
            self.add(tag_up, up_src, up_dst, {"gx": up_x}, inner_end, inner_start)
            return self.add(tag_down, down_src, down_dst, {"gx": down_x}, inner_start, inner_end)

        def span(self, tag, src, above, below):
            self.add(tag, src, above, {"gy": up_y})
            if sides == 2:
                self.add(tag, src, below, {"gy": down_y})
            return self

        def start(self, *tags):
            for tag, copy, out_if, _ in self.items:
                if tag in tags:
                    if out_if is None:
                        copy().start()
                    else:
                        pl.when(out_if)(lambda: copy().start())

        def wait(self):
            for _, copy, out_if, in_if in self.items:
                if out_if is None:
                    copy().wait()
                else:
                    pl.when(out_if)(lambda: copy().wait_send())
                    pl.when(in_if)(lambda: copy().wait_recv())

    above = sides

    def ids_exchange():
        return Exchange(i_s, i_r).span("s", ID.at[0], ID.at[1], ID.at[above])

    def fields_exchange():
        e = Exchange(a_s, a_r)
        e.rows("r", "r", F.at[:, R, mid], F.at[:, 0, mid], F.at[:, 1, mid], F.at[:, R + 1, mid])
        return e.span("s", EA.at[0], EA.at[1], EA.at[above]).span("s", NM.at[0], NM.at[1], NM.at[above])

    def speed_exchange():
        return Exchange(b_s, b_r).rows("r", "r", U.at[R], U.at[0], U.at[1], U.at[R + 1])

    def source_exchange():
        e = Exchange(c_s, c_r)
        for side, to in ((0, up_y), (1, down_y))[:sides]:
            e.add(blocks - 1, EC.at[blocks - 1], EL.at[side, 0], {"gx": up_x, "gy": to}, inner_end, inner_start)
            e.add(0, EC.at[0], EL.at[side, tiles - 1], {"gx": down_x, "gy": to}, inner_start, inner_end)
        e.rows(
            blocks - 1, 0,
            RR.at[pl.ds(R, H), mid], RR.at[pl.ds(0, H), mid],
            RR.at[pl.ds(H, H), mid], RR.at[pl.ds(H + R, H), mid])
        for b in range(blocks):
            e.span(b, EC.at[b], EL.at[0, b + 1], EL.at[above - 1, b + 1])
        return e.rows(blocks - 1, 0, EC.at[blocks - 1], XE.at[0], EC.at[0], XE.at[1])

    def planes_copy(d):
        return pltpu.make_async_remote_copy(
            src_ref=planes, dst_ref=PL.at[pl.ds(lay * held, held)],
            send_sem=p_s.at[d], recv_sem=p_r.at[d],
            device_id={"layout": lax.rem(lay + d, NL)}, device_id_type=MESH,
        )

    def planes_landing(d):
        source = lax.rem(lay + NL - d, NL)
        return pltpu.make_async_remote_copy(
            src_ref=planes, dst_ref=PL.at[pl.ds(source * held, held)],
            send_sem=p_s.at[d], recv_sem=p_r.at[d],
            device_id={"layout": source}, device_id_type=MESH,
        )

    ids_exchange().start("s")

    @pl.when(first)
    def _():
        for d in range(1, NL):
            planes_copy(d).start()

    lane = lax.broadcasted_iota(jnp.int32, (K, 128), 1)
    level = lax.broadcasted_iota(jnp.int32, (K, 128), 0)
    at_first, at_last = lane == 0, lane == 127
    odd_lane = lax.rem(lane, 2) == 1
    low = K // 2 - RADIUS
    in_band = (level >= low) & (level <= low + 2 * RADIUS)
    lane_8 = lax.broadcasted_iota(jnp.int32, (8, 128), 1)
    level_8 = lax.broadcasted_iota(jnp.int32, (8, 128), 0)
    first_8, last_8 = lane_8 == 0, lane_8 == 127
    place = lax.rem(lane, 16)
    group = lane // 16
    early = place < 8

    def beside_8(f, rim):
        return pltpu.roll(jnp.where(last_8, rim, f), 1, 1), pltpu.roll(jnp.where(first_8, rim, f), 127, 1)

    def put(ref, index, f):
        ref[(*index, mid)] = f
        ref[(*index, pl.ds(7, 1))] = f[0:1]
        ref[(*index, pl.ds(8 + K, 1))] = f[K - 1:K]

    def level_pair(ref, index):
        return ref[(*index, pl.ds(7, K))], ref[(*index, pl.ds(9, K))]

    own_ids = ID[0]
    cosines = jnp.zeros((R, 128), jnp.float32)
    sines, runs = cosines, cosines
    for t in range(turbines):
        here = own_ids == t
        cosines = jnp.where(here, table[0, t], cosines)
        sines = jnp.where(here, table[1, t], sines)
        runs = jnp.where(here, table[2, t], runs)
    FO[2] = cosines
    FO[3] = sines
    FO[4] = runs

    lane_r = lax.broadcasted_iota(jnp.int32, (R, 128), 1)
    shifts = []
    for shift in range(1, 2 * RADIUS + 1):
        shifts.append((1, shift, lane_r >= 128 - shift))
        shifts.append((above, 128 - shift, lane_r < shift))

    def disk_masks():
        names = [ID[0], ID[1], ID[above]]
        for i, (other, amount, wraps) in enumerate(shifts):
            there = names[1] if other == 1 else names[2]
            i_sh = pltpu.roll(jnp.where(wraps, there, names[0]), amount, 1)
            MK[i] = jnp.where(i_sh == names[0], 1.0, 0.0)

    def disk_forces():
        own, before, after = NM[0], NM[1], NM[above]
        total = own
        for i, (other, amount, wraps) in enumerate(shifts):
            n_sh = pltpu.roll(jnp.where(wraps, before if i % 2 == 0 else after, own), amount, 1)
            total = total + jnp.where(MK[i] > 0.5, n_sh, 0.0)
        speed = total / float((2 * RADIUS + 1) ** 2)
        thrust = (-0.5 * THRUST_COEFF * TIME_STEP) * speed * jnp.abs(speed) * FO[4]
        FO[0] = thrust * FO[2]
        FO[1] = thrust * FO[3]

    def disk_sums(row, u, v):
        SU[0, row:row + 1, :] = jnp.sum(jnp.where(in_band, u, 0.0), axis=0, keepdims=True)
        SU[1, row:row + 1, :] = jnp.sum(jnp.where(in_band, v, 0.0), axis=0, keepdims=True)

    def send_span():
        NM[0] = SU[0] * FO[2] + SU[1] * FO[3]
        fields_exchange().start("s")

    width = 128 // groups

    def theta_copy(par, d):
        return pltpu.make_async_remote_copy(
            src_ref=TS.at[par, 0], dst_ref=TS.at[par, d],
            send_sem=t_s.at[par, d], recv_sem=t_r.at[par, d],
            device_id=device_of(lax.rem(s + d, N)), device_id_type=MESH,
        )

    def send_theta(par, total):
        packed = jnp.zeros((8, 128), jnp.float32)
        for g in range(groups):
            part = jnp.sum(total[g * 8:(g + 1) * 8], axis=1, keepdims=True)
            packed = jnp.where(lane_8 // width == g, part, packed)
        TS[par, 0] = packed
        for d in range(1, N):
            theta_copy(par, d).start()

    def mean_theta(par):
        for d in range(1, N):
            theta_copy(par, d).wait()
        total = TS[par, 0]
        for d in range(1, N):
            total = total + TS[par, d]
        total = total * (TIME_STEP * BUOYANCY / columns)
        for g in range(groups):
            MB[8 * g:8 * g + 8] = jnp.broadcast_to(total[:, g * width:g * width + 1], (8, 128))

    def pack2(packed, f, j):
        return jnp.where(lane // 2 == j, pltpu.roll(f, 2 * j + 1, 1), packed)

    def pack16(packed, f, j):
        return jnp.where(group == j, pltpu.roll(f, (16 * j + 8) % 128, 1), packed)

    def unpack16(packed, j):
        return pltpu.roll(packed, (120 - 16 * j) % 128, 1)

    own_theta.wait()
    total = zero
    packed = zero
    for row in range(R):
        warm = T[row + 1, mid] + prof[1]
        put(T, (row + 1,), warm)
        if row in (0, R - 1):
            F[3, row + 1, mid] = warm
        packed = pack2(packed, warm, 3 * R + row)
        total = total + warm
    send_theta(0, total)
    own_state.wait()
    for row in range(R):
        u = F[0, row + 1, mid] + prof[0]
        v = F[1, row + 1, mid]
        put(F, (0, row + 1), u)
        put(F, (1, row + 1), v)
        disk_sums(row, u, v)
        for c, f in enumerate((u, v, F[2, row + 1, mid])):
            packed = pack2(packed, f, c * R + row)
    EA[0] = packed
    fields_exchange().start("r")
    send_span()
    ids_exchange().wait()
    disk_masks()

    @pl.when(first)
    def _():
        own_planes.wait()
        for d in range(1, NL):
            planes_copy(d).wait_send()
            planes_landing(d).wait_recv()

    def rim_of(rims, j):
        return pltpu.roll(rims, 127 - 2 * j, 1)

    def tendency_row(row):
        x = row + 1
        for g in range(groups):
            k = 8 + 8 * g
            rims = EM[8 * g:8 * g + 8]
            cen, dx, dy, dz, around = [], [], [], [], []
            for c in range(3):
                f = F[c, x, k:k + 8]
                xm, xp = F[c, x - 1, k:k + 8], F[c, x + 1, k:k + 8]
                ym, yp = beside_8(f, rim_of(rims, c * R + row))
                km, kp = F[c, x, k - 1:k + 7], F[c, x, k + 1:k + 9]
                cen.append(f)
                dx.append(xp - xm)
                dy.append(yp - ym)
                dz.append(kp - km)
                around.append((xp + xm) + (kp + km) + (yp + ym))
            square = 2.0 * (dx[0] * dx[0] + dy[1] * dy[1] + dz[2] * dz[2])
            for shear in (dy[0] + dx[1], dz[0] + dx[2], dz[1] + dy[2]):
                square = square + shear * shear
            nu = (TIME_STEP * VISCOSITY) + (0.5 * TIME_STEP * SMAGORINSKY) * jnp.sqrt(square)
            NU[row, 8 * g:8 * g + 8] = nu
            remain = 1.0 - 6.0 * nu
            half_u, half_v, half_w = ((0.5 * TIME_STEP) * f for f in cen)
            for c in range(3):
                new = (cen[c] * remain + around[c] * nu) - (half_u * dx[c] + half_v * dy[c] + half_w * dz[c])
                if c < 2:
                    if 8 * g <= low + 2 * RADIUS and 8 * g + 7 >= low:
                        at = level_8 + 8 * g
                        band = (at >= low) & (at <= low + 2 * RADIUS)
                        force = FO[c, pl.ds(row, 1), :]
                        new = new + jnp.where(band, jnp.broadcast_to(force, (8, 128)), 0.0)
                else:
                    new = new + ((TIME_STEP * BUOYANCY) * T[x, k:k + 8] - MB[8 * g:8 * g + 8])
                if c == 0:
                    U[x, 8 * g:8 * g + 8] = new
                elif c == 1:
                    V[row, 8 * g:8 * g + 8] = new
                else:
                    W[row, k:k + 8] = new

    def theta_row(row):
        x = row + 1
        parts = []
        for g in range(groups):
            k = 8 + 8 * g
            f = T[x, k:k + 8]
            xm, xp = T[x - 1, k:k + 8], T[x + 1, k:k + 8]
            ym, yp = beside_8(f, rim_of(EM[8 * g:8 * g + 8], 3 * R + row))
            km, kp = T[x, k - 1:k + 7], T[x, k + 1:k + 9]
            nu = DIFFUSIVITY_RATIO * NU[row, 8 * g:8 * g + 8]
            turn = F[0, x, k:k + 8] * (xp - xm) + F[1, x, k:k + 8] * (yp - ym) + F[2, x, k:k + 8] * (kp - km)
            new = f * (1.0 - 6.0 * nu) + ((xp + xm) + (kp + km) + (yp + ym)) * nu - (0.5 * TIME_STEP) * turn
            TH[row, 8 * g:8 * g + 8] = new
            parts.append(new)
        return parts

    def sources():
        for b in range(blocks):
            packed = zero
            rims = zero
            for j in range(8):
                row = 8 * b + j
                v = V[row]
                v_next = pltpu.roll(v, 1, 1)
                vm = jnp.where(at_first, 0.0, v_next)
                vp = jnp.where(at_last, 0.0, pltpu.roll(v, 127, 1))
                wm, wp = level_pair(W, (row,))
                r = ((U[row + 2] - U[row]) + (vp - vm) + (wp - wm)) * 0.5
                RR[row + H, mid] = r
                packed = pack16(packed, r, j)
                rims = jnp.where(group == j, pltpu.roll(v_next, 16 * j, 1) if j else v_next, rims)
            OC[b] = packed
            EC[b] = jnp.where(place < 2, rims, packed)
            source_exchange().start(b)

    def row_places(t):
        if t == 0:
            return [(i, 8 - H + i) for i in range(H)]
        if t == tiles - 1:
            return [(R + H + i, i) for i in range(H)]
        return [(8 * (t - 1) + j + H, j) for j in range(8)]

    def complete():
        for t in range(tiles):
            if t in (0, tiles - 1):
                clean = zero
                for x, j in row_places(t):
                    clean = pack16(clean, RR[x, mid], j)
                own = XE[0 if t == 0 else 1]
            else:
                clean, own = OC[t - 1], EC[t - 1]
            before, after = EL[0, t], EL[above - 1, t]
            left = jnp.where(early, before, clean)
            left = left + 0.5 * jnp.where(place == 7, pltpu.roll(own, 6, 1), 0.0)
            left = left - 0.5 * jnp.where(place == 8, pltpu.roll(before, 8, 1), 0.0)
            right = jnp.where(early, clean, after)
            right = right + 0.5 * jnp.where(place == 7, pltpu.roll(after, 6, 1), 0.0)
            right = right - 0.5 * jnp.where(place == 8, pltpu.roll(own, 8, 1), 0.0)
            put(SR, (0, t), left)
            put(SR, (1, t), right)
            whole = jnp.where(early, right, left)
            for x, j in row_places(t):
                put(RR, (x,), jnp.where(at_first | at_last, unpack16(whole, j), RR[x, mid]))

    sixth = jnp.float32(1.0 / 6.0)
    at_start = jnp.where(first, 0.0, sixth).astype(jnp.float32)
    at_end = jnp.where(last, 0.0, sixth).astype(jnp.float32)

    def relax(index, around, centre, source, keep):
        if index == 0:
            return (around * (-1.0 / 6.0) - centre) * keep
        return (around - source) * keep

    def sweep(index, v):
        old = RR if index == 0 else PP[(index - 1) % 2]
        new = PP[index % 2]
        for x in range(H - (v - 1), R + H + (v - 1)):
            keep = at_start if x < H else at_end if x >= R + H else sixth
            for g in range(groups):
                k = 8 + 8 * g
                f = old[x, k:k + 8]
                around = (old[x + 1, k:k + 8] + old[x - 1, k:k + 8])
                around = around + (old[x, k - 1:k + 7] + old[x, k + 1:k + 9])
                around = around + (pltpu.roll(f, 1, 1) + pltpu.roll(f, 127, 1))
                p = relax(index, around, f, RR[x, k:k + 8] if index else None, keep)
                new[x, k:k + 8] = p
                if g == 0:
                    new[x, 7:8] = p[0:1]
                if g == groups - 1:
                    new[x, 8 + K:9 + K] = p[7:8]
        old = SR if index == 0 else SS[(index - 1) % 2]
        new = SS[index % 2]
        for side in range(2):
            for t in range(tiles):
                keep = at_start if t == 0 else at_end if t == tiles - 1 else sixth
                f = old[side, t, mid]
                fm = old[side, t - 1, mid] if t else f
                fp = old[side, t + 1, mid] if t < tiles - 1 else f
                km, kp = level_pair(old, (side, t))
                around = pltpu.roll(jnp.where(group == 7, fm, f), 16, 1)
                around = around + pltpu.roll(jnp.where(group == 0, fp, f), 112, 1)
                around = around + (km + kp) + (pltpu.roll(f, 1, 1) + pltpu.roll(f, 127, 1))
                put(new, (side, t), relax(index, around, f, SR[side, t, mid] if index else None, keep))

    def finish(n):
        p, side = PP[(SWEEPS - 1) % 2], SS[(SWEEPS - 1) % 2]
        edge = (lane < SWEEPS) | (lane >= 128 - SWEEPS)
        wholes, rims = [], []
        for t in range(tiles):
            left, right = side[0, t, mid], side[1, t, mid]
            wholes.append(jnp.where(early, right, left))
            rims.append(jnp.where(early, left, right))

        def merge(x, t, j):
            put(p, (x,), jnp.where(edge, unpack16(wholes[t], j), p[x, mid]))

        merge(H - 1, 0, 7)
        merge(R + H, tiles - 1, 0)
        for row in range(R):
            merge(row + H, row // 8 + 1, row % 8)
        packed = zero
        for row in [0, R - 1] + list(range(1, R - 1)):
            x = row + H
            centre = p[x, mid]
            rim = unpack16(rims[row // 8 + 1], row % 8)
            ym = pltpu.roll(jnp.where(at_last, rim, centre), 1, 1)
            yp = pltpu.roll(jnp.where(at_first, rim, centre), 127, 1)
            km, kp = level_pair(p, (x,))
            u = U[row + 1] - 0.5 * (p[x + 1, mid] - p[x - 1, mid])
            v = V[row] - 0.5 * (yp - ym)
            w = W[row, mid] - 0.5 * (kp - km)
            warm = TH[row]
            disk_sums(row, u, v)
            put(F, (0, row + 1), u)
            put(F, (1, row + 1), v)
            F[2, row + 1, mid] = w
            put(T, (row + 1,), warm)
            if row in (0, R - 1):
                F[3, row + 1, mid] = warm
            for c, f in enumerate((u, v, w, warm)):
                packed = pack2(packed, f, c * R + row)
            if row == R - 1:
                pl.when(n < STEPS - 1)(lambda: fields_exchange().start("r"))
        EA[0] = packed

    def step(n, carry):
        par = lax.rem(n, 2)
        fields_exchange().wait()

        @pl.when(first)
        def _():
            plane = slot[n]
            for c in range(4):
                f = PL[plane, c]
                if c in (0, 3):
                    f = f + prof[0 if c == 0 else 1]
                F[c, 0, mid] = f
                if c == 0:
                    U[0] = f

        @pl.when(last)
        def _():
            for c in range(4):
                F[c, R + 1, mid] = F[c, R, mid]

        T[0, mid] = F[3, 0, mid]
        T[R + 1, mid] = F[3, R + 1, mid]
        EM[...] = jnp.where(odd_lane, EA[above], EA[1])
        disk_forces()
        mean_theta(par)

        def pair(i, c):
            tendency_row(i)
            tendency_row(R - 1 - i)
            pl.when(i == 0)(lambda: speed_exchange().start("r"))
            return c

        lax.fori_loop(0, R // 2, pair, 0)

        @pl.when(last)
        def _():
            U[R + 1] = U[R]

        speed_exchange().wait()
        sources()

        def warm_row(row, parts):
            return tuple(a + b for a, b in zip(parts, theta_row(row)))

        parts = lax.fori_loop(0, R, warm_row, tuple(no_level for _ in range(groups)))

        @pl.when(n < STEPS - 1)
        def _():
            send_theta(1 - par, jnp.concatenate(parts, axis=0))

        source_exchange().wait()
        complete()
        for i in range(SWEEPS):
            sweep(i, H - i)
        finish(n)

        @pl.when(n < STEPS - 1)
        def _():
            send_span()

        return carry

    lax.fori_loop(0, STEPS, step, 0)

    own_out = pltpu.make_async_copy(F.at[pl.ds(0, 3), pl.ds(1, R), mid], out.at[0, pl.ds(0, 3)], loc.at[2])
    theta_out = pltpu.make_async_copy(T.at[pl.ds(1, R), mid], out.at[0, 3], loc.at[4])
    own_out.start()
    theta_out.start()
    own_out.wait()
    theta_out.wait()


def solution(mesh):
    NL, GX, L = mesh.shape["layout"], mesh.shape["gx"], mesh.shape["gy"]

    def local(state, planes, turbine_cell, active, yaw_sector, slot):
        rows, K, cols = state.shape[2:]
        R = rows
        H = SWEEPS + 1
        N = GX * L
        turbines = active.shape[1]
        KP, tiles, sides = K + 16, R // 8 + 2, 1 if L == 2 else 2
        held = planes.shape[0]
        ids = turbine_cell[0, :, K // 2, :]
        angle = (yaw_sector[0].astype(jnp.float32) - 3.5) * YAW_INCREMENT
        table = jnp.stack([jnp.cos(angle), jnp.sin(angle), active[0].astype(jnp.float32)])
        prof = jnp.broadcast_to(profiles(K)[:, :, None], (2, K, cols))
        smem = pl.BlockSpec(memory_space=pltpu.SMEM)
        vmem = pl.BlockSpec(memory_space=pltpu.VMEM)
        hbm = pl.BlockSpec(memory_space=pl.ANY)
        f32 = jnp.float32
        dma = pltpu.SemaphoreType.DMA
        return pl.pallas_call(
            functools.partial(
                kernel, NL, GX, L, R, K, H, turbines, held, float(rows * GX * cols * L)
            ),
            out_shape=jax.ShapeDtypeStruct(state.shape, f32),
            in_specs=[smem, smem, vmem, vmem, hbm, hbm],
            out_specs=hbm,
            scratch_shapes=[
                pltpu.VMEM((4, R + 2, KP, cols), f32),
                pltpu.VMEM((R + 2, KP, cols), f32),
                pltpu.VMEM((R, K, cols), f32),
                pltpu.VMEM((R, K, cols), f32),
                pltpu.VMEM((R, K, cols), f32),
                pltpu.VMEM((R, KP, cols), f32),
                pltpu.VMEM((R + 2, K, cols), f32),
                pltpu.VMEM((R + 2 * H, KP, cols), f32),
                pltpu.VMEM((R + 2 * H, KP, cols), f32),
                pltpu.VMEM((R + 2 * H, KP, cols), f32),
                pltpu.VMEM((2, tiles, KP, cols), f32),
                pltpu.VMEM((2, tiles, KP, cols), f32),
                pltpu.VMEM((2, tiles, KP, cols), f32),
                pltpu.VMEM((held * NL, 4, K, cols), f32),
                pltpu.VMEM((sides + 1, R, cols), jnp.int32),
                pltpu.VMEM((2, R, cols), f32),
                pltpu.VMEM((sides + 1, R, cols), f32),
                pltpu.VMEM((5, R, cols), f32),
                pltpu.VMEM((4 * RADIUS, R, cols), f32),
                pltpu.VMEM((2, N, 8, 128), f32),
                pltpu.VMEM((sides + 1, K, cols), f32),
                pltpu.VMEM((K, cols), f32),
                pltpu.VMEM((K, cols), f32),
                pltpu.VMEM((R // 8, K, cols), f32),
                pltpu.VMEM((R // 8, K, cols), f32),
                pltpu.VMEM((sides, tiles, K, cols), f32),
                pltpu.VMEM((2, K, cols), f32),
                dma((2,)), dma((2,)), dma((NL,)), dma((NL,)),
                dma((6,)), dma((6,)), dma((2,)), dma((2,)),
                dma((4 + sides * tiles,)), dma((4 + sides * tiles,)),
                dma((2, N)), dma((2, N)),
                dma((5,)),
            ],
            compiler_params=pltpu.CompilerParams(
                collective_id=0, has_side_effects=True, vmem_limit_bytes=40 * 1024 * 1024
            ),
        )(slot, table, prof, ids, state, planes)

    return jax.shard_map(
        local,
        mesh=mesh,
        in_specs=(
            P("layout", None, "gx", None, "gy"),
            P("layout", None, None, "gy"),
            P("layout", "gx", None, "gy"),
            P("layout", None),
            P("layout", None),
            P(),
        ),
        out_specs=P("layout", None, "gx", None, "gy"),
        check_vma=False,
    )
```

time: 78.8 us -> 65.9 us (0.84)
  Pallas kernels: 73.2 us -> 60.3 us
    pallas_call x1, Pallas kernels: 73.2 us -> 60.3 us  [local(): pl.pallas_call(functools.partial(kernel, NL, GX, L, R, K, H, turbines, he...]
where the time goes in v1:
time: 65.9 us; the launch traced here: 65.7 us
  Pallas kernels  60.3 us (92%)
  local copies, waits for them, and re-layouts  4.61 us (7%)
  other arithmetic  0.75 us (1%)
    pallas_call x1, Pallas kernels, local(): pl.pallas_call(functools.partial(kernel, NL, GX, L, R, K, H, turbines, he...  60.3 us
    unnamed x9, local copies, waits for them, and re-layouts  3.69 us

profile of v1, /device:TPU:1, one launch (start us, length us, event | category | flops | bytes accessed | tf_op | source)
XLA Modules:
  0.0 65.7 jit_solution(13506797166563187475)
XLA Ops:
  0.0 0.0 copy-start.3
  0.0 0.7 %convert_element_type.26 = f32[1,16]{1,0:T(1,128)S(1)} convert(s32[1,16]{1,0:T(1,128)} %param.9) | non-fusion elementwise | flops 16 | bytes 128 | tf_op jit(solution)/shard_map/convert_element_type | solution.py:608
  0.7 0.0 copy-done.3
  0.8 0.8 %slice.3 = s32[1,16,1,128]{3,2,1,0:T(1,128)S(1)} slice(s32[1,16,32,128]{3,2,1,0:T(8,128)} %param.8), slice={[0:1], [0:16], [16:17], [0:128]} | slice | bytes 16384 | tf_op jit(solution)/shard_map/slice | solution.py:606
  1.6 0.0 copy-start.2
  1.6 0.1 broadcast_in_dim.2.prof
  1.7 0.6 copy-done.2
  2.3 0.0 copy-start
  2.3 1.2 %copy-done = f32[1,4,16,32,128]{4,3,2,1,0:T(8,128)S(1)} copy-done((f32[1,4,16,32,128]{4,3,2,1,0:T(8,128)S(1)}, f32[1,4,16,32,128]{4,3,2,1,0:T(8,128)}, u32[]{:S(2)}) %copy-start) | copy-done | bytes 1048600
  3.5 0.0 copy-start.1
  3.5 0.9 %copy-done.1 = f32[2,4,32,128]{3,2,1,0:T(8,128)S(1)} copy-done((f32[2,4,32,128]{3,2,1,0:T(8,128)S(1)}, f32[2,4,32,128]{3,2,1,0:T(8,128)}, u32[]{:S(2)}) %copy-start.1) | copy-done | bytes 131096
  4.4 60.3 %shard_map.64 = f32[1,4,16,32,128]{4,3,2,1,0:T(8,128)S(1)} custom-call(s32[4]{0:T(128)S(1)} %copy-done.2, f32[3,16]{1,0:T(4,128)S(1)} %pad_maximum_fusion.table, f32[2,32,128]{2,1,0:T(8,128)S(1)} %broadcast_in_dim.2.prof, s32[16,128]{1,0:T(8,128)S(1)} %bitcast.3, f32[1,4,16,32,128]{4,3,2,1,0:T(8,128)S(1)} %copy-done, f32[2,4,32,128]{3,2,1,0:T(8,128)S(1)} %copy-done.1), custom_call_target="tpu_custom_call" | custom-call | tf_op jit(solution)/shard_map/pallas_call | solution.py:615
  64.7 1.0 %copy.10 = f32[1,4,16,32,128]{4,3,2,1,0:T(8,128)} copy(f32[1,4,16,32,128]{4,3,2,1,0:T(8,128)S(1)} %shard_map.64) | data formatting | bytes 2097152
  (4 shorter events, 0.1 us)
Async XLA Ops:
  0.0 0.7 %copy-start.3 = (s32[1,16]{1,0:T(1,128)S(1)}, s32[1,16]{1,0:T(1,128)}, u32[]{:S(2)}) copy-start(s32[1,16]{1,0:T(1,128)} %param.10) | copy-start | bytes 196
  1.6 0.7 copy-start.2
  2.3 1.2 %copy-start = (f32[1,4,16,32,128]{4,3,2,1,0:T(8,128)S(1)}, f32[1,4,16,32,128]{4,3,2,1,0:T(8,128)}, u32[]{:S(2)}) copy-start(f32[1,4,16,32,128]{4,3,2,1,0:T(8,128)} %state.1) | copy-start | bytes 3145732
  3.5 0.9 %copy-start.1 = (f32[2,4,32,128]{3,2,1,0:T(8,128)S(1)}, f32[2,4,32,128]{3,2,1,0:T(8,128)}, u32[]{:S(2)}) copy-start(f32[2,4,32,128]{3,2,1,0:T(8,128)} %planes.1) | copy-start | bytes 393220

commit v2 on v1

--- a/solution.py
+++ b/solution.py
@@ -30,7 +30,7 @@
     NL, GX, L, R, K, H, turbines, held, columns,
     slot, table, prof, ids, state, planes,
     out,
-    F, T, TH, NU, V, W, U, RR, PA, PB, SR, SA, SB, PL, ID, SU, NM, FO, MK, TS, EA, EM, MB, OC, EC, EL, XE,
+    F, T, TH, NU, V, W, U, RR, PA, PB, SR, SA, SB, PL, ID, SU, NM, FO, MK, TS, EA, EM, MB, OC, EC, EL, XE, HP, P0,
     i_s, i_r, p_s, p_r, a_s, a_r, b_s, b_r, c_s, c_r, t_s, t_r, loc,
 ):
     lay = lax.axis_index("layout")
@@ -69,11 +69,13 @@
     own_state = pltpu.make_async_copy(state.at[0, pl.ds(0, 3)], F.at[pl.ds(0, 3), pl.ds(1, R), mid], loc.at[0])
     own_theta = pltpu.make_async_copy(state.at[0, 3], T.at[pl.ds(1, R), mid], loc.at[3])
     own_planes = pltpu.make_async_copy(planes, PL.at[pl.ds(lay * held, held)], loc.at[1])
+    held_planes = pltpu.make_async_copy(planes, HP, loc.at[5])
     own_state.start()
     own_theta.start()
 
     @pl.when(first)
     def _():
+        held_planes.start()
         own_planes.start()
 
     zero = jnp.zeros((K, 128), jnp.float32)
@@ -187,10 +189,23 @@
             device_id={"layout": source}, device_id_type=MESH,
         )
 
+    def first_plane(d, source):
+        return pltpu.make_async_remote_copy(
+            src_ref=P0.at[lay], dst_ref=P0.at[source],
+            send_sem=p_s.at[NL + d], recv_sem=p_r.at[NL + d],
+            device_id={"layout": lax.rem(lay + d, NL)}, device_id_type=MESH,
+        )
+
     ids_exchange().start("s")
 
     @pl.when(first)
     def _():
+        held_planes.wait()
+        near = jnp.minimum(jnp.maximum(slot[0] - lay * held, 0), held - 1)
+        for c in range(4):
+            P0[lay, c] = HP[near, c]
+        for d in range(1, NL):
+            first_plane(d, lay).start()
         for d in range(1, NL):
             planes_copy(d).start()
 
@@ -202,13 +217,14 @@
     in_band = (level >= low) & (level <= low + 2 * RADIUS)
     lane_8 = lax.broadcasted_iota(jnp.int32, (8, 128), 1)
     level_8 = lax.broadcasted_iota(jnp.int32, (8, 128), 0)
-    first_8, last_8 = lane_8 == 0, lane_8 == 127
-    place = lax.rem(lane, 16)
-    group = lane // 16
+    around_end = lax.rem(lane + 1, 128)
+    window = lax.rem(lane + 8, 128)
+    place = lax.rem(window, 16)
+    group = window // 16
     early = place < 8
 
-    def beside_8(f, rim):
-        return pltpu.roll(jnp.where(last_8, rim, f), 1, 1), pltpu.roll(jnp.where(first_8, rim, f), 127, 1)
+    def beside(f, rim):
+        return pltpu.roll(jnp.where(at_last, rim, f), 1, 1), pltpu.roll(jnp.where(at_first, rim, f), 127, 1)
 
     def put(ref, index, f):
         ref[(*index, mid)] = f
@@ -290,61 +306,58 @@
         for g in range(groups):
             MB[8 * g:8 * g + 8] = jnp.broadcast_to(total[:, g * width:g * width + 1], (8, 128))
 
-    def pack2(packed, f, j):
-        return jnp.where(lane // 2 == j, pltpu.roll(f, 2 * j + 1, 1), packed)
-
-    def pack16(packed, f, j):
-        return jnp.where(group == j, pltpu.roll(f, (16 * j + 8) % 128, 1), packed)
+    def gather(items, place_of, width):
+        while len(items) > 1:
+            merged = []
+            for a, b in zip(items[::2], items[1::2]):
+                if a is None and b is None:
+                    merged.append(None)
+                    continue
+                moved = zero if b is None else pltpu.roll(b, width, 1)
+                merged.append(jnp.where(place_of < width, zero if a is None else a, moved))
+            items, width = merged, 2 * width
+        return items[0]
 
     def unpack16(packed, j):
-        return pltpu.roll(packed, (120 - 16 * j) % 128, 1)
+        return pltpu.roll(packed, 128 - 16 * j, 1) if j else packed
 
     own_theta.wait()
     total = zero
-    packed = zero
     for row in range(R):
         warm = T[row + 1, mid] + prof[1]
         put(T, (row + 1,), warm)
         if row in (0, R - 1):
             F[3, row + 1, mid] = warm
-        packed = pack2(packed, warm, 3 * R + row)
         total = total + warm
     send_theta(0, total)
     own_state.wait()
+    rims = []
     for row in range(R):
         u = F[0, row + 1, mid] + prof[0]
         v = F[1, row + 1, mid]
         put(F, (0, row + 1), u)
         put(F, (1, row + 1), v)
         disk_sums(row, u, v)
-        for c, f in enumerate((u, v, F[2, row + 1, mid])):
-            packed = pack2(packed, f, c * R + row)
-    EA[0] = packed
+        rims.append(gather([u, v, F[2, row + 1, mid], T[row + 1, mid]], around_end, 2))
+    EA[0] = gather(rims, around_end, 8)
     fields_exchange().start("r")
     send_span()
     ids_exchange().wait()
     disk_masks()
 
-    @pl.when(first)
-    def _():
-        own_planes.wait()
-        for d in range(1, NL):
-            planes_copy(d).wait_send()
-            planes_landing(d).wait_recv()
-
-    def rim_of(rims, j):
-        return pltpu.roll(rims, 127 - 2 * j, 1)
+    def rim_of(row, c):
+        return pltpu.roll(EM[...], lax.rem(128 - 8 * row - 2 * c, 128), 1)
 
     def tendency_row(row):
         x = row + 1
+        y_pairs = [beside(F[c, x, mid], rim_of(row, c)) for c in range(3)]
         for g in range(groups):
             k = 8 + 8 * g
-            rims = EM[8 * g:8 * g + 8]
             cen, dx, dy, dz, around = [], [], [], [], []
             for c in range(3):
                 f = F[c, x, k:k + 8]
                 xm, xp = F[c, x - 1, k:k + 8], F[c, x + 1, k:k + 8]
-                ym, yp = beside_8(f, rim_of(rims, c * R + row))
+                ym, yp = (f_y[8 * g:8 * g + 8] for f_y in y_pairs[c])
                 km, kp = F[c, x, k - 1:k + 7], F[c, x, k + 1:k + 9]
                 cen.append(f)
                 dx.append(xp - xm)
@@ -377,12 +390,13 @@
 
     def theta_row(row):
         x = row + 1
+        y_pair = beside(T[x, mid], rim_of(row, 3))
         parts = []
         for g in range(groups):
             k = 8 + 8 * g
             f = T[x, k:k + 8]
             xm, xp = T[x - 1, k:k + 8], T[x + 1, k:k + 8]
-            ym, yp = beside_8(f, rim_of(EM[8 * g:8 * g + 8], 3 * R + row))
+            ym, yp = (f_y[8 * g:8 * g + 8] for f_y in y_pair)
             km, kp = T[x, k - 1:k + 7], T[x, k + 1:k + 9]
             nu = DIFFUSIVITY_RATIO * NU[row, 8 * g:8 * g + 8]
             turn = F[0, x, k:k + 8] * (xp - xm) + F[1, x, k:k + 8] * (yp - ym) + F[2, x, k:k + 8] * (kp - km)
@@ -393,8 +407,7 @@
 
     def sources():
         for b in range(blocks):
-            packed = zero
-            rims = zero
+            rows, rims = [], []
             for j in range(8):
                 row = 8 * b + j
                 v = V[row]
@@ -404,10 +417,11 @@
                 wm, wp = level_pair(W, (row,))
                 r = ((U[row + 2] - U[row]) + (vp - vm) + (wp - wm)) * 0.5
                 RR[row + H, mid] = r
-                packed = pack16(packed, r, j)
-                rims = jnp.where(group == j, pltpu.roll(v_next, 16 * j, 1) if j else v_next, rims)
+                rows.append(r)
+                rims.append(v_next)
+            packed = gather(rows, window, 16)
             OC[b] = packed
-            EC[b] = jnp.where(place < 2, rims, packed)
+            EC[b] = jnp.where(place < 2, pltpu.roll(gather(rims, lane, 16), 120, 1), packed)
             source_exchange().start(b)
 
     def row_places(t):
@@ -418,11 +432,11 @@
         return [(8 * (t - 1) + j + H, j) for j in range(8)]
 
     def complete():
+        wholes = []
         for t in range(tiles):
             if t in (0, tiles - 1):
-                clean = zero
-                for x, j in row_places(t):
-                    clean = pack16(clean, RR[x, mid], j)
+                known = dict((j, x) for x, j in row_places(t))
+                clean = gather([RR[known[j], mid] if j in known else None for j in range(8)], window, 16)
                 own = XE[0 if t == 0 else 1]
             else:
                 clean, own = OC[t - 1], EC[t - 1]
@@ -435,9 +449,12 @@
             right = right - 0.5 * jnp.where(place == 8, pltpu.roll(own, 8, 1), 0.0)
             put(SR, (0, t), left)
             put(SR, (1, t), right)
-            whole = jnp.where(early, right, left)
-            for x, j in row_places(t):
-                put(RR, (x,), jnp.where(at_first | at_last, unpack16(whole, j), RR[x, mid]))
+            wholes.append(jnp.where(early, right, left))
+        for slot_j in range(8):
+            for t in range(tiles):
+                for x, j in row_places(t):
+                    if j == slot_j:
+                        put(RR, (x,), jnp.where(at_first | at_last, unpack16(wholes[t], j), RR[x, mid]))
 
     sixth = jnp.float32(1.0 / 6.0)
     at_start = jnp.where(first, 0.0, sixth).astype(jnp.float32)
@@ -493,13 +510,15 @@
 
         merge(H - 1, 0, 7)
         merge(R + H, tiles - 1, 0)
-        for row in range(R):
-            merge(row + H, row // 8 + 1, row % 8)
-        packed = zero
+        for j in range(8):
+            for b in range(blocks):
+                merge(8 * b + j + H, b + 1, j)
+                RR[8 * b + j + H, mid] = unpack16(rims[b + 1], j)
+        rows = [None] * R
         for row in [0, R - 1] + list(range(1, R - 1)):
             x = row + H
             centre = p[x, mid]
-            rim = unpack16(rims[row // 8 + 1], row % 8)
+            rim = RR[x, mid]
             ym = pltpu.roll(jnp.where(at_last, rim, centre), 1, 1)
             yp = pltpu.roll(jnp.where(at_first, rim, centre), 127, 1)
             km, kp = level_pair(p, (x,))
@@ -514,27 +533,42 @@
             put(T, (row + 1,), warm)
             if row in (0, R - 1):
                 F[3, row + 1, mid] = warm
-            for c, f in enumerate((u, v, w, warm)):
-                packed = pack2(packed, f, c * R + row)
+            rows[row] = gather([u, v, w, warm], around_end, 2)
             if row == R - 1:
                 pl.when(n < STEPS - 1)(lambda: fields_exchange().start("r"))
-        EA[0] = packed
+        EA[0] = gather(rows, around_end, 8)
 
     def step(n, carry):
         par = lax.rem(n, 2)
         fields_exchange().wait()
 
-        @pl.when(first)
-        def _():
-            plane = slot[n]
+        def inflow(held_in, index):
             for c in range(4):
-                f = PL[plane, c]
+                f = held_in[index, c]
                 if c in (0, 3):
                     f = f + prof[0 if c == 0 else 1]
                 F[c, 0, mid] = f
                 if c == 0:
                     U[0] = f
 
+        @pl.when(first & (n == 0))
+        def _():
+            for d in range(1, NL):
+                first_plane(d, lay).wait_send()
+                first_plane(d, lax.rem(lay + NL - d, NL)).wait_recv()
+            inflow(P0, lax.div(slot[0], held))
+
+        @pl.when(first & (n == 1))
+        def _():
+            own_planes.wait()
+            for d in range(1, NL):
+                planes_copy(d).wait_send()
+                planes_landing(d).wait_recv()
+
+        @pl.when(first & (n > 0))
+        def _():
+            inflow(PL, slot[n])
+
         @pl.when(last)
         def _():
             for c in range(4):
@@ -542,7 +576,7 @@
 
         T[0, mid] = F[3, 0, mid]
         T[R + 1, mid] = F[3, R + 1, mid]
-        EM[...] = jnp.where(odd_lane, EA[above], EA[1])
+        EM[...] = jnp.where(odd_lane, EA[1], EA[above])
         disk_forces()
         mean_theta(par)
 
@@ -564,7 +598,8 @@
         def warm_row(row, parts):
             return tuple(a + b for a, b in zip(parts, theta_row(row)))
 
-        parts = lax.fori_loop(0, R, warm_row, tuple(no_level for _ in range(groups)))
+        parts = lax.fori_loop(
+            0, R // 2, lambda i, c: warm_row(2 * i + 1, warm_row(2 * i, c)), tuple(no_level for _ in range(groups)))
 
         @pl.when(n < STEPS - 1)
         def _():
@@ -647,14 +682,16 @@
                 pltpu.VMEM((R // 8, K, cols), f32),
                 pltpu.VMEM((sides, tiles, K, cols), f32),
                 pltpu.VMEM((2, K, cols), f32),
-                dma((2,)), dma((2,)), dma((NL,)), dma((NL,)),
+                pltpu.VMEM((held, 4, K, cols), f32),
+                pltpu.VMEM((NL, 4, K, cols), f32),
+                dma((2,)), dma((2,)), dma((2 * NL,)), dma((2 * NL,)),
                 dma((6,)), dma((6,)), dma((2,)), dma((2,)),
                 dma((4 + sides * tiles,)), dma((4 + sides * tiles,)),
                 dma((2, N)), dma((2, N)),
-                dma((5,)),
+                dma((6,)),
             ],
             compiler_params=pltpu.CompilerParams(
-                collective_id=0, has_side_effects=True, vmem_limit_bytes=40 * 1024 * 1024
+                collective_id=0, has_side_effects=True, vmem_limit_bytes=60 * 1024 * 1024
             ),
         )(slot, table, prof, ids, state, planes)
 

time: 65.9 us -> 64.9 us (0.985)
  Pallas kernels: 60.3 us -> 58.7 us
    pallas_call x1, Pallas kernels: 60.3 us -> 58.7 us  [local(): pl.pallas_call(functools.partial(kernel, NL, GX, L, R, K, H, turbines, he...]
    unnamed x9 -> x3, local copies, waits for them, and re-layouts: 3.69 us -> 2.27 us
where the time goes in v2:
time: 64.9 us; the launch traced here: 64.4 us
  Pallas kernels  58.7 us (90%)
  local copies, waits for them, and re-layouts  4.4 us (7%)
  other arithmetic  1.34 us (2%)
    pallas_call x1, Pallas kernels, local(): pl.pallas_call(functools.partial(kernel, NL, GX, L, R, K, H, turbines, he...  58.7 us
    unnamed x3, local copies, waits for them, and re-layouts  2.27 us
    slice x1, local copies, waits for them, and re-layouts, local(): ids = turbine_cell[0, :, K // 2, :]  1.44 us

profile of v2, /device:TPU:1, one launch (start us, length us, event | category | flops | bytes accessed | tf_op | source)
XLA Modules:
  0.0 64.4 jit_solution(3665209587290774679)
XLA Ops:
  0.0 0.0 copy-start
  0.0 0.7 %convert_element_type.26 = f32[1,16]{1,0:T(1,128)S(1)} convert(s32[1,16]{1,0:T(1,128)} %param.9) | non-fusion elementwise | flops 16 | bytes 128 | tf_op jit(solution)/shard_map/convert_element_type | solution.py:643
  0.7 0.0 copy-done
  0.7 0.6 pad_maximum_fusion.table
  1.4 1.4 %slice.3 = s32[1,16,1,128]{3,2,1,0:T(1,128)} slice(s32[1,16,32,128]{3,2,1,0:T(8,128)} %param.8), slice={[0:1], [0:16], [16:17], [0:128]} | slice | bytes 16384 | tf_op jit(solution)/shard_map/slice | solution.py:641
  2.8 0.7 %broadcast_in_dim.2.prof = f32[2,32,128]{2,1,0:T(8,128)} broadcast(f32[2,32]{1,0:T(2,128)S(1)} %pad_maximum_fusion.1), dimensions={0,1} | broadcast | bytes 33024 | tf_op jit(solution)/shard_map/broadcast_in_dim | solution.py:644
  3.5 58.7 %shard_map.64 = f32[1,4,16,32,128]{4,3,2,1,0:T(8,128)} custom-call(s32[4]{0:T(128)} %slot.1, f32[3,16]{1,0:T(4,128)} %pad_maximum_fusion.table, f32[2,32,128]{2,1,0:T(8,128)} %broadcast_in_dim.2.prof, s32[16,128]{1,0:T(8,128)} %bitcast.3, f32[1,4,16,32,128]{4,3,2,1,0:T(8,128)} %state.1, f32[2,4,32,128]{3,2,1,0:T(8,128)} %planes.1), custom_call_target="tpu_custom_call" | custom-call | tf_op jit(solution)/shard_map/pallas_call | solution.py:650
  62.2 2.3 %copy.10 = f32[1,4,16,32,128]{4,3,2,1,0:T(8,128)} copy(f32[1,4,16,32,128]{4,3,2,1,0:T(8,128)} %shard_map.64) | data formatting | bytes 2097152
  (3 shorter events, 0.1 us)
Async XLA Ops:
  0.0 0.7 %copy-start = (s32[1,16]{1,0:T(1,128)S(1)}, s32[1,16]{1,0:T(1,128)}, u32[]{:S(2)}) copy-start(s32[1,16]{1,0:T(1,128)} %param.10) | copy-start | bytes 196

commit v3 on v2

--- a/solution.py
+++ b/solution.py
@@ -21,16 +21,11 @@
 MESH = pl.DeviceIdType.MESH
 
 
-def profiles(levels):
-    height = (jnp.arange(levels).astype(jnp.float32) + 0.5) / levels
-    return jnp.stack([height ** (1.0 / 7.0), 0.5 * height])
-
-
 def kernel(
     NL, GX, L, R, K, H, turbines, held, columns,
-    slot, table, prof, ids, state, planes,
+    slot, active, yaw_sector, cells, state, planes,
     out,
-    F, T, TH, NU, V, W, U, RR, PA, PB, SR, SA, SB, PL, ID, SU, NM, FO, MK, TS, EA, EM, MB, OC, EC, EL, XE, HP, P0,
+    F, T, TH, NU, V, W, U, RR, PA, PB, SR, SA, SB, PL, ID, SU, NM, FO, MK, TS, EA, EM, MB, OC, EC, EL, XE, HP, P0, prof,
     i_s, i_r, p_s, p_r, a_s, a_r, b_s, b_r, c_s, c_r, t_s, t_r, loc,
 ):
     lay = lax.axis_index("layout")
@@ -70,8 +65,10 @@
     own_theta = pltpu.make_async_copy(state.at[0, 3], T.at[pl.ds(1, R), mid], loc.at[3])
     own_planes = pltpu.make_async_copy(planes, PL.at[pl.ds(lay * held, held)], loc.at[1])
     held_planes = pltpu.make_async_copy(planes, HP, loc.at[5])
+    own_ids_copy = pltpu.make_async_copy(cells.at[0, :, K // 2], ID.at[0], loc.at[6])
+    own_ids_copy.start()
+    own_theta.start()
     own_state.start()
-    own_theta.start()
 
     @pl.when(first)
     def _():
@@ -96,6 +93,9 @@
             EL[i, tiles - 1] = zero
         XE[1] = zero
 
+    height = (lax.broadcasted_iota(jnp.int32, (K, 128), 0).astype(jnp.float32) + 0.5) * (1.0 / K)
+    prof[0] = jnp.exp(jnp.log(height) * (1.0 / 7.0))
+    prof[1] = 0.5 * height
     no_level = jnp.zeros((8, 128), jnp.float32)
     for row in range(R):
         W[row, 0:8] = no_level
@@ -103,7 +103,7 @@
         F[2, row + 1, 0:8] = no_level
         F[2, row + 1, 8 + K:16 + K] = no_level
 
-    ID[0] = ids[...]
+    own_ids_copy.wait()
 
     pl.semaphore_wait(barrier, N - 1 + jnp.where(first, NL - 1, 0))
 
@@ -235,16 +235,16 @@
         return ref[(*index, pl.ds(7, K))], ref[(*index, pl.ds(9, K))]
 
     own_ids = ID[0]
-    cosines = jnp.zeros((R, 128), jnp.float32)
-    sines, runs = cosines, cosines
+    sectors = jnp.zeros((R, 128), jnp.int32)
+    runs = sectors
     for t in range(turbines):
         here = own_ids == t
-        cosines = jnp.where(here, table[0, t], cosines)
-        sines = jnp.where(here, table[1, t], sines)
-        runs = jnp.where(here, table[2, t], runs)
-    FO[2] = cosines
-    FO[3] = sines
-    FO[4] = runs
+        sectors = jnp.where(here, yaw_sector[0, t], sectors)
+        runs = jnp.where(here, active[0, t], runs)
+    angle = (sectors.astype(jnp.float32) - 3.5) * YAW_INCREMENT
+    FO[2] = jnp.where(own_ids >= 0, jnp.cos(angle), 0.0)
+    FO[3] = jnp.where(own_ids >= 0, jnp.sin(angle), 0.0)
+    FO[4] = runs.astype(jnp.float32)
 
     lane_r = lax.broadcasted_iota(jnp.int32, (R, 128), 1)
     shifts = []
@@ -638,13 +638,9 @@
         turbines = active.shape[1]
         KP, tiles, sides = K + 16, R // 8 + 2, 1 if L == 2 else 2
         held = planes.shape[0]
-        ids = turbine_cell[0, :, K // 2, :]
-        angle = (yaw_sector[0].astype(jnp.float32) - 3.5) * YAW_INCREMENT
-        table = jnp.stack([jnp.cos(angle), jnp.sin(angle), active[0].astype(jnp.float32)])
-        prof = jnp.broadcast_to(profiles(K)[:, :, None], (2, K, cols))
         smem = pl.BlockSpec(memory_space=pltpu.SMEM)
-        vmem = pl.BlockSpec(memory_space=pltpu.VMEM)
-        hbm = pl.BlockSpec(memory_space=pl.ANY)
+        hbm = pl.BlockSpec(memory_space=pltpu.HBM)
+        free = pl.BlockSpec(memory_space=pl.ANY)
         f32 = jnp.float32
         dma = pltpu.SemaphoreType.DMA
         return pl.pallas_call(
@@ -652,8 +648,8 @@
                 kernel, NL, GX, L, R, K, H, turbines, held, float(rows * GX * cols * L)
             ),
             out_shape=jax.ShapeDtypeStruct(state.shape, f32),
-            in_specs=[smem, smem, vmem, vmem, hbm, hbm],
-            out_specs=hbm,
+            in_specs=[smem, smem, smem, hbm, hbm, hbm],
+            out_specs=free,
             scratch_shapes=[
                 pltpu.VMEM((4, R + 2, KP, cols), f32),
                 pltpu.VMEM((R + 2, KP, cols), f32),
@@ -684,16 +680,17 @@
                 pltpu.VMEM((2, K, cols), f32),
                 pltpu.VMEM((held, 4, K, cols), f32),
                 pltpu.VMEM((NL, 4, K, cols), f32),
+                pltpu.VMEM((2, K, cols), f32),
                 dma((2,)), dma((2,)), dma((2 * NL,)), dma((2 * NL,)),
                 dma((6,)), dma((6,)), dma((2,)), dma((2,)),
                 dma((4 + sides * tiles,)), dma((4 + sides * tiles,)),
                 dma((2, N)), dma((2, N)),
-                dma((6,)),
+                dma((7,)),
             ],
             compiler_params=pltpu.CompilerParams(
                 collective_id=0, has_side_effects=True, vmem_limit_bytes=60 * 1024 * 1024
             ),
-        )(slot, table, prof, ids, state, planes)
+        )(slot, active, yaw_sector, turbine_cell, state, planes)
 
     return jax.shard_map(
         local,

time: 64.9 us -> 61.2 us (0.943)
  local copies, waits for them, and re-layouts: 4.4 us -> 2.26 us
  other arithmetic: 1.34 us -> 0 us
    slice x1 -> x0, local copies, waits for them, and re-layouts: 1.44 us -> none  [local(): ids = turbine_cell[0, :, K // 2, :]]
    broadcast_in_dim x1 -> x0, local copies, waits for them, and re-layouts: 0.69 us -> none  [local(): prof = jnp.broadcast_to(profiles(K)[:, :, None], (2, K, cols))]
    convert_element_type x1 -> x0, other arithmetic: 0.67 us -> none  [local(): active[0].astype(jnp.float32)]
    unnamed x3 -> x1, local copies, waits for them, and re-layouts: 2.27 us -> 2.26 us
where the time goes in v3:
time: 61.2 us; the launch traced here: 60.9 us
  Pallas kernels  58.6 us (96%)
  local copies, waits for them, and re-layouts  2.26 us (4%)
    pallas_call x1, Pallas kernels, local(): pl.pallas_call(functools.partial(kernel, NL, GX, L, R, K, H, turbines, he...  58.6 us
    unnamed x1, local copies, waits for them, and re-layouts  2.26 us

profile of v3, /device:TPU:1, one launch (start us, length us, event | category | flops | bytes accessed | tf_op | source)
XLA Modules:
  0.0 60.9 jit_solution(10380129214145307870)
XLA Ops:
  0.0 58.6 %shard_map.64 = f32[1,4,16,32,128]{4,3,2,1,0:T(8,128)} custom-call(s32[4]{0:T(128)} %slot.1, s32[1,16]{1,0:T(1,128)} %active.1, s32[1,16]{1,0:T(1,128)} %yaw_sector.1, s32[1,16,32,128]{3,2,1,0:T(8,128)} %cells.1, f32[1,4,16,32,128]{4,3,2,1,0:T(8,128)} %state.1, f32[2,4,32,128]{3,2,1,0:T(8,128)} %planes.1), custom_call_target="tpu_custom_call" | custom-call | tf_op jit(solution)/shard_map/pallas_call | solution.py:646
  58.6 2.3 %copy.8 = f32[1,4,16,32,128]{4,3,2,1,0:T(8,128)} copy(f32[1,4,16,32,128]{4,3,2,1,0:T(8,128)} %shard_map.64) | data formatting | bytes 2097152
